TPU v7x, 512 devices: a whole 4x4x16 slice. The times are simulated.
512 devices in a mesh: dp: 64 (over y, z), mp: 8 (over x, core).
Axes of the slice: x: 4, y: 4, z: 16, core: 2. Of those that a mesh axis runs over, the one named last changes fastest.
Arguments:
- tokens_in: bfloat16 [8192, 8192], P('dp', 'mp'), may hold values from -6 to 6
- gate_pre: bfloat16 [8192, 28672], P('dp', 'mp'), may hold values from -8 to 8
- up_pre: bfloat16 [8192, 28672], P('dp', 'mp'), may hold values from -6 to 6
- hidden_grad: bfloat16 [8192, 28672], P('dp', 'mp'), may hold values from -160 to 160
- out_grad: bfloat16 [8192, 8192], P('dp', 'mp'), may hold values from -160 to 160
- proj_model: bfloat16 [8192, 128], P('mp'), may hold values from -0.0625 to 0.0625
- proj_hidden: bfloat16 [28672, 128], P('mp'), may hold values from -0.03125 to 0.03125
Outputs:
- whitened: float32 [64, 128, 64], P('dp', 'mp')
All inputs are finite; a program needn't handle non-finite values.
Results may differ from a plain program's by a relative error of at most 0.003.
Values sent between devices are 32-bit elements; how exact they have to be, the bound alone decides.
A program may use at most 64 MiB of HBM per device.

v0:
```python
import math
import jax
import jax.numpy as jnp
from jax import lax
from jax.sharding import PartitionSpec as P

RANK = 64
LEN = 128
highest = lax.Precision.HIGHEST


def partner_2(value, axis, apart):
    mask = 2**apart
    pairs = [(source, source ^ mask) for source in range(lax.axis_size(axis))]
    return lax.ppermute(value, axis, pairs)


def gradient_blocks(projected):
    columns_each = projected.shape[-1] // 4
    input_side = projected[..., :columns_each]
    output_side = projected[..., columns_each : 2 * columns_each]
    upward = projected[..., 2 * columns_each : 3 * columns_each]
    hidden_side = projected[..., 3 * columns_each :]
    up_block = jnp.einsum("elr,els->ers", input_side, upward, precision=highest)
    down_block = jnp.einsum("elr,els->ers", hidden_side, output_side, precision=highest)
    return jnp.concatenate([up_block, down_block], axis=1)


def gram_of(rows):
    flat_rows = rows.reshape(-1, rows.shape[-1])
    return jnp.dot(flat_rows.T, flat_rows, precision=highest, preferred_element_type=jnp.float32)


def shards(tokens_in, gate_pre, up_pre, hidden_grad, out_grad, proj_model, proj_hidden):
    gate_act = jax.nn.silu(gate_pre.astype(jnp.float32))
    up_grad = (hidden_grad.astype(jnp.float32) * gate_act).astype(jnp.bfloat16)
    hidden = (gate_act * up_pre.astype(jnp.float32)).astype(jnp.bfloat16)
    local_sums = jnp.concatenate(
        [
            jnp.dot(tokens_in, proj_model[:, :RANK], preferred_element_type=jnp.float32),
            jnp.dot(out_grad, proj_model[:, RANK:], preferred_element_type=jnp.float32),
            jnp.dot(up_grad, proj_hidden[:, :RANK], preferred_element_type=jnp.float32),
            jnp.dot(hidden, proj_hidden[:, RANK:], preferred_element_type=jnp.float32),
        ],
        axis=1,
    )
    local_examples = tokens_in.shape[0] // LEN
    shaped = local_sums.reshape(local_examples, LEN, 4 * RANK)
    model_shards = lax.axis_size("mp")
    rows_each = 2 * RANK // model_shards
    summed = lax.psum(shaped, "mp")
    blocks = gradient_blocks(summed)
    mine = lax.dynamic_slice_in_dim(blocks, lax.axis_index("mp") * rows_each, rows_each, 1)
    group_gram = gram_of(blocks)
    flat_mine = mine.reshape(local_examples * rows_each, RANK)
    lower = jnp.linalg.cholesky(group_gram)
    for level in range(lax.axis_size("dp").bit_length() - 1):
        partner = partner_2(lower, "dp", level)
        combined = jnp.dot(
            lower, lower.T, precision=highest, preferred_element_type=jnp.float32
        ) + jnp.dot(partner, partner.T, precision=highest, preferred_element_type=jnp.float32)
        lower = jnp.linalg.cholesky(combined)
    solved = jax.scipy.linalg.solve_triangular(lower, flat_mine.T, lower=True)
    factor = math.sqrt(local_examples * lax.axis_size("dp") * 2 * RANK)
    return (solved.T * factor).reshape(local_examples, rows_each, RANK)


def solution(mesh):
    in_specs = (
        P("dp", "mp"),
        P("dp", "mp"),
        P("dp", "mp"),
        P("dp", "mp"),
        P("dp", "mp"),
        P("mp", None),
        P("mp", None),
    )
    out_specs = P("dp", "mp", None)
    return jax.shard_map(shards, mesh=mesh, in_specs=in_specs, out_specs=out_specs, check_vma=False)
```

profile of v0, /device:TPU:8, one launch (start us, length us, event | category | flops | bytes accessed | tf_op | source)
XLA Modules:
  0.0 209.8 jit_solution(459969425136288152)
XLA Ops:
  6.6 2.7 %fusion.4 = f32[128,64]{0,1:T(8,128)S(1)} fusion(bf16[128,3584]{1,0:T(8,128)(2,1)} %param.11, bf16[3584,128]{1,0:T(8,128)(2,1)} %param.14, bf16[128,3584]{1,0:T(8,128)(2,1)} %param.9), kind=kOutput, calls=%fused_computation.17 | convolution fusion | flops 62390272 | bytes 2785280 | tf_op jit(solution)/shard_map/dot_general | solution.py:42
  9.3 1.0 fusion.5
  11.7 79.8 %all-reduce.2.cloned.1.call-done = f32[1,128,256]{1,2,0:T(8,128)} async-done(((f32[1,128,256]{1,2,0:T(8,128)}), f32[1,128,256]{1,2,0:T(8,128)}) %all-reduce.2.cloned.1.call-update) | async-done | bytes 131088 | tf_op jit(solution)/shard_map/psum | solution.py:51
  92.5 1.0 convolution_bitcast_fusion.1
  93.8 5.8 %cholesky.119 = f32[64,64]{1,0:T(8,128)S(1)} custom-call(f32[64,64]{1,0:T(8,128)S(1)} %fusion.23), custom_call_target="Cholesky" | custom-call | tf_op jit(solution)/shard_map/jit(cholesky)/cholesky | solution.py:56
  101.0 3.5 %collective-permute-start = (f32[64,64]{1,0:T(8,128)S(1)}, f32[64,64]{1,0:T(8,128)S(1)}, u32[]{:S(2)}, u32[]{:S(2)}) collective-permute-start(f32[64,64]{1,0:T(8,128)S(1)} %select_select_fusion.6), channel_id=1, source_target_pairs={{0,8},{8,0},{16,24},{24,16},{32,40},{40,32},{48,56},{56,48},{64,72... | collective-permute-start | bytes 49160 | tf_op jit(solution)/shard_map/ppermute | solution.py:15
  104.6 2.1 %collective-permute-done = f32[64,64]{1,0:T(8,128)S(1)} collective-permute-done((f32[64,64]{1,0:T(8,128)S(1)}, f32[64,64]{1,0:T(8,128)S(1)}, u32[]{:S(2)}, u32[]{:S(2)}) %collective-permute-start) | collective-permute-done | bytes 16416 | tf_op jit(solution)/shard_map/ppermute | solution.py:15
  107.1 5.8 %cholesky.130 = f32[64,64]{1,0:T(8,128)S(1)} custom-call(f32[64,64]{1,0:T(8,128)S(1)} %fusion.22), custom_call_target="Cholesky" | custom-call | tf_op jit(solution)/shard_map/jit(cholesky)/cholesky | solution.py:62
  114.3 4.5 %collective-permute-start.1 = (f32[64,64]{1,0:T(8,128)S(1)}, f32[64,64]{1,0:T(8,128)S(1)}, u32[]{:S(2)}, u32[]{:S(2)}) collective-permute-start(f32[64,64]{1,0:T(8,128)S(1)} %select_select_fusion.5), channel_id=1, source_target_pairs={{0,16},{8,24},{16,0},{24,8},{32,48},{40,56},{48,32},{56,40},{64,80... | collective-permute-start | bytes 49160 | tf_op jit(solution)/shard_map/ppermute | solution.py:15
  118.9 2.1 collective-permute-done.1
  121.2 5.8 %cholesky.141 = f32[64,64]{1,0:T(8,128)S(1)} custom-call(f32[64,64]{1,0:T(8,128)S(1)} %fusion.21), custom_call_target="Cholesky" | custom-call | tf_op jit(solution)/shard_map/jit(cholesky)/cholesky | solution.py:62
  128.4 7.6 %collective-permute-start.2 = (f32[64,64]{1,0:T(8,128)S(1)}, f32[64,64]{1,0:T(8,128)S(1)}, u32[]{:S(2)}, u32[]{:S(2)}) collective-permute-start(f32[64,64]{1,0:T(8,128)S(1)} %select_select_fusion.4), channel_id=1, source_target_pairs={{0,32},{8,40},{16,48},{24,56},{32,0},{40,8},{48,16},{56,24},{64,96... | collective-permute-start | bytes 49160 | tf_op jit(solution)/shard_map/ppermute | solution.py:15
  136.3 1.9 collective-permute-done.2
  138.4 5.8 %cholesky.152 = f32[64,64]{1,0:T(8,128)S(1)} custom-call(f32[64,64]{1,0:T(8,128)S(1)} %fusion.20), custom_call_target="Cholesky" | custom-call | tf_op jit(solution)/shard_map/jit(cholesky)/cholesky | solution.py:62
  145.6 14.1 %collective-permute-start.3 = (f32[64,64]{1,0:T(8,128)S(1)}, f32[64,64]{1,0:T(8,128)S(1)}, u32[]{:S(2)}, u32[]{:S(2)}) collective-permute-start(f32[64,64]{1,0:T(8,128)S(1)} %select_select_fusion.3), channel_id=1, source_target_pairs={{0,64},{8,72},{16,80},{24,88},{32,96},{40,104},{48,112},{56,120},{... | collective-permute-start | bytes 49160 | tf_op jit(solution)/shard_map/ppermute | solution.py:15
  159.9 1.7 collective-permute-done.3
  161.9 5.8 %cholesky.163 = f32[64,64]{1,0:T(8,128)S(1)} custom-call(f32[64,64]{1,0:T(8,128)S(1)} %fusion.19), custom_call_target="Cholesky" | custom-call | tf_op jit(solution)/shard_map/jit(cholesky)/cholesky | solution.py:62
  169.1 2.4 %collective-permute-start.4 = (f32[64,64]{1,0:T(8,128)S(1)}, f32[64,64]{1,0:T(8,128)S(1)}, u32[]{:S(2)}, u32[]{:S(2)}) collective-permute-start(f32[64,64]{1,0:T(8,128)S(1)} %select_select_fusion.2), channel_id=1, source_target_pairs={{0,128},{8,136},{16,144},{24,152},{32,160},{40,168},{48,176},{56,1... | collective-permute-start | bytes 49160 | tf_op jit(solution)/shard_map/ppermute | solution.py:15
  171.7 3.2 %collective-permute-done.4 = f32[64,64]{1,0:T(8,128)S(1)} collective-permute-done((f32[64,64]{1,0:T(8,128)S(1)}, f32[64,64]{1,0:T(8,128)S(1)}, u32[]{:S(2)}, u32[]{:S(2)}) %collective-permute-start.4) | collective-permute-done | bytes 16416 | tf_op jit(solution)/shard_map/ppermute | solution.py:15
  175.2 5.8 %cholesky.174 = f32[64,64]{1,0:T(8,128)S(1)} custom-call(f32[64,64]{1,0:T(8,128)S(1)} %fusion.18), custom_call_target="Cholesky" | custom-call | tf_op jit(solution)/shard_map/jit(cholesky)/cholesky | solution.py:62
  182.4 4.0 %collective-permute-start.5 = (f32[64,64]{1,0:T(8,128)S(1)}, f32[64,64]{1,0:T(8,128)S(1)}, u32[]{:S(2)}, u32[]{:S(2)}) collective-permute-start(f32[64,64]{1,0:T(8,128)S(1)} %select_select_fusion.1), channel_id=1, source_target_pairs={{0,256},{8,264},{16,272},{24,280},{32,288},{40,296},{48,304},{56,3... | collective-permute-start | bytes 49160 | tf_op jit(solution)/shard_map/ppermute | solution.py:15
  186.6 3.1 %collective-permute-done.5 = f32[64,64]{1,0:T(8,128)S(1)} collective-permute-done((f32[64,64]{1,0:T(8,128)S(1)}, f32[64,64]{1,0:T(8,128)S(1)}, u32[]{:S(2)}, u32[]{:S(2)}) %collective-permute-start.5) | collective-permute-done | bytes 16416 | tf_op jit(solution)/shard_map/ppermute | solution.py:15
  190.0 5.8 %cholesky.185 = f32[64,64]{1,0:T(8,128)S(1)} custom-call(f32[64,64]{1,0:T(8,128)S(1)} %fusion.17), custom_call_target="Cholesky" | custom-call | tf_op jit(solution)/shard_map/jit(cholesky)/cholesky | solution.py:62
  197.2 4.9 %custom-call.6 = f32[1,64,64]{1,2,0:T(8,128)S(1)} custom-call(f32[1,64,64]{2,1,0:T(8,128)S(1)} %fusion.12), custom_call_target="InvertDiagBlocksLowerTriangular" | custom-call | tf_op jit(solution)/shard_map/jit(_solve_triangular)/triangular_solve | solution.py:63
  (67 shorter events, 15.6 us)
Async XLA Ops:
  6.5 3.8 %copy-start = (bf16[128,1024]{1,0:T(8,128)(2,1)S(1)}, bf16[128,1024]{1,0:T(8,128)(2,1)}, u32[]{:S(2)}) copy-start(bf16[128,1024]{1,0:T(8,128)(2,1)} %param.8) | copy-start | bytes 786436
  6.5 2.7 %copy-start.4 = (bf16[3584,128]{1,0:T(8,128)(2,1)S(1)}, bf16[3584,128]{1,0:T(8,128)(2,1)}, u32[]{:S(2)}) copy-start(bf16[3584,128]{1,0:T(8,128)(2,1)} %param.14) | copy-start | bytes 2752516
  6.5 2.7 %copy-start.5 = (bf16[128,3584]{1,0:T(8,128)(2,1)S(1)}, bf16[128,3584]{1,0:T(8,128)(2,1)}, u32[]{:S(2)}) copy-start(bf16[128,3584]{1,0:T(8,128)(2,1)} %param.9) | copy-start | bytes 2752516
  6.5 2.7 %copy-start.3 = (bf16[128,3584]{1,0:T(8,128)(2,1)S(1)}, bf16[128,3584]{1,0:T(8,128)(2,1)}, u32[]{:S(2)}) copy-start(bf16[128,3584]{1,0:T(8,128)(2,1)} %param.10) | copy-start | bytes 2752516
  6.5 85.0 %all-reduce.2.cloned.1.call-start = ((), (), s32[]{:S(2)}) async-start(), calls=%async_computation | async-start | bytes 262144 | tf_op jit(solution)/shard_map/psum | solution.py:51
  9.3 1.0 copy-start.1
  9.3 1.3 copy-start.2
  101.0 5.8 %collective-permute-start = (f32[64,64]{1,0:T(8,128)S(1)}, f32[64,64]{1,0:T(8,128)S(1)}, u32[]{:S(2)}, u32[]{:S(2)}) collective-permute-start(f32[64,64]{1,0:T(8,128)S(1)} %select_select_fusion.6), channel_id=1, source_target_pairs={{0,8},{8,0},{16,24},{24,16},{32,40},{40,32},{48,56},{56,48},{64,72... | collective-permute-start | bytes 49160 | tf_op jit(solution)/shard_map/ppermute | solution.py:15
  114.3 6.7 %collective-permute-start.1 = (f32[64,64]{1,0:T(8,128)S(1)}, f32[64,64]{1,0:T(8,128)S(1)}, u32[]{:S(2)}, u32[]{:S(2)}) collective-permute-start(f32[64,64]{1,0:T(8,128)S(1)} %select_select_fusion.5), channel_id=1, source_target_pairs={{0,16},{8,24},{16,0},{24,8},{32,48},{40,56},{48,32},{56,40},{64,80... | collective-permute-start | bytes 49160 | tf_op jit(solution)/shard_map/ppermute | solution.py:15
  128.4 9.7 %collective-permute-start.2 = (f32[64,64]{1,0:T(8,128)S(1)}, f32[64,64]{1,0:T(8,128)S(1)}, u32[]{:S(2)}, u32[]{:S(2)}) collective-permute-start(f32[64,64]{1,0:T(8,128)S(1)} %select_select_fusion.4), channel_id=1, source_target_pairs={{0,32},{8,40},{16,48},{24,56},{32,0},{40,8},{48,16},{56,24},{64,96... | collective-permute-start | bytes 49160 | tf_op jit(solution)/shard_map/ppermute | solution.py:15
  145.6 16.0 %collective-permute-start.3 = (f32[64,64]{1,0:T(8,128)S(1)}, f32[64,64]{1,0:T(8,128)S(1)}, u32[]{:S(2)}, u32[]{:S(2)}) collective-permute-start(f32[64,64]{1,0:T(8,128)S(1)} %select_select_fusion.3), channel_id=1, source_target_pairs={{0,64},{8,72},{16,80},{24,88},{32,96},{40,104},{48,112},{56,120},{... | collective-permute-start | bytes 49160 | tf_op jit(solution)/shard_map/ppermute | solution.py:15
  169.1 5.8 %collective-permute-start.4 = (f32[64,64]{1,0:T(8,128)S(1)}, f32[64,64]{1,0:T(8,128)S(1)}, u32[]{:S(2)}, u32[]{:S(2)}) collective-permute-start(f32[64,64]{1,0:T(8,128)S(1)} %select_select_fusion.2), channel_id=1, source_target_pairs={{0,128},{8,136},{16,144},{24,152},{32,160},{40,168},{48,176},{56,1... | collective-permute-start | bytes 49160 | tf_op jit(solution)/shard_map/ppermute | solution.py:15
  182.4 7.3 %collective-permute-start.5 = (f32[64,64]{1,0:T(8,128)S(1)}, f32[64,64]{1,0:T(8,128)S(1)}, u32[]{:S(2)}, u32[]{:S(2)}) collective-permute-start(f32[64,64]{1,0:T(8,128)S(1)} %select_select_fusion.1), channel_id=1, source_target_pairs={{0,256},{8,264},{16,272},{24,280},{32,288},{40,296},{48,304},{56,3... | collective-permute-start | bytes 49160 | tf_op jit(solution)/shard_map/ppermute | solution.py:15
Sparse Core Ops, SparseCore 0:
  11.8 79.6 all-reduce.1
where the time goes:
time: 210 us
  waiting for transfers between devices  93.9 us (45%)
  other arithmetic  55.8 us (27%)
  starting transfers between devices  36.1 us (17%)
  between operations  13.8 us (7%)
  matrix products  9.57 us (5%)
    psum x1, waiting for transfers between devices, shards(): summed = lax.psum(shaped, 'mp')  79.8 us
    another operation x18, other arithmetic, shards(): lower = jnp.linalg.cholesky(combined)  39.1 us
    ppermute x6, starting transfers between devices, partner_2(): return lax.ppermute(value, axis, pairs)  36.1 us
    ppermute x6, waiting for transfers between devices, partner_2(): return lax.ppermute(value, axis, pairs)  14.1 us
    another operation x3, other arithmetic, shards(): lower = jnp.linalg.cholesky(group_gram)  6.52 us
    another operation x2, other arithmetic, shards(): solved = jax.scipy.linalg.solve_triangular(lower, flat_mine.T, lower=True)  5.55 us
  transfers between devices with their start and end apart: 7, of which 7 were waited for; matrix products, arithmetic and copies ran while one was open for 1% of the time, Pallas kernels for 0%

commit v1 on v0

--- a/solution.py
+++ b/solution.py
@@ -48,7 +48,7 @@
     shaped = local_sums.reshape(local_examples, LEN, 4 * RANK)
     model_shards = lax.axis_size("mp")
     rows_each = 2 * RANK // model_shards
-    summed = lax.psum(shaped, "mp")
+    summed = jnp.sum(lax.all_gather(shaped, "mp"), axis=0)
     blocks = gradient_blocks(summed)
     mine = lax.dynamic_slice_in_dim(blocks, lax.axis_index("mp") * rows_each, rows_each, 1)
     group_gram = gram_of(blocks)

time: 210 us -> 166 us (0.79)
  waiting for transfers between devices: 93.9 us -> 49.5 us
    psum x1 -> x0, waiting for transfers between devices: 79.8 us -> none  [shards(): summed = lax.psum(shaped, 'mp')]
    all_gather x0 -> x1, waiting for transfers between devices: none -> 35.5 us  [shards(): summed = jnp.sum(lax.all_gather(shaped, 'mp'), axis=0)]
where the time goes in v1:
time: 166 us
  other arithmetic  56.1 us (34%)
  waiting for transfers between devices  49.5 us (30%)
  starting transfers between devices  36.1 us (22%)
  between operations  13.8 us (8%)
  matrix products  8.03 us (5%)
  local copies, waits for them, and re-layouts  1.97 us (1%)
    another operation x18, other arithmetic, shards(): lower = jnp.linalg.cholesky(combined)  39.1 us
    ppermute x6, starting transfers between devices, partner_2(): return lax.ppermute(value, axis, pairs)  36.1 us
    all_gather x1, waiting for transfers between devices, shards(): summed = jnp.sum(lax.all_gather(shaped, 'mp'), axis=0)  35.5 us
    ppermute x6, waiting for transfers between devices, partner_2(): return lax.ppermute(value, axis, pairs)  14 us
    another operation x3, other arithmetic, shards(): lower = jnp.linalg.cholesky(group_gram)  6.52 us
    another operation x2, other arithmetic, shards(): solved = jax.scipy.linalg.solve_triangular(lower, flat_mine.T, lower=True)  5.55 us
  transfers between devices with their start and end apart: 7, of which 7 were waited for; matrix products, arithmetic and copies ran while one was open for 1% of the time, Pallas kernels for 0%

profile of v1, /device:TPU:8, one launch (start us, length us, event | category | flops | bytes accessed | tf_op | source)
XLA Modules:
  0.0 165.5 jit_solution(14622303164799292180)
XLA Ops:
  6.6 2.7 %fusion.4 = f32[128,64]{0,1:T(8,128)S(1)} fusion(bf16[128,3584]{1,0:T(8,128)(2,1)} %param.11, bf16[3584,128]{1,0:T(8,128)(2,1)} %param.14, bf16[128,3584]{1,0:T(8,128)(2,1)} %param.9), kind=kOutput, calls=%fused_computation.18 | convolution fusion | flops 62390272 | bytes 2785280 | tf_op jit(solution)/shard_map/dot_general | solution.py:42
  9.3 1.0 fusion.5
  11.7 35.5 %all-gather.3.cloned.1.call-done = f32[1024,256]{0,1:T(8,128)} async-done(((f32[128,256]{0,1:T(8,128)}), f32[1024,256]{0,1:T(8,128)}) %all-gather.3.cloned.1.call-update) | async-done | bytes 1048592 | tf_op jit(solution)/shard_map/all_gather | solution.py:51
  47.1 1.4 copy.58
  49.5 5.8 %cholesky.119 = f32[64,64]{1,0:T(8,128)S(1)} custom-call(f32[64,64]{1,0:T(8,128)S(1)} %fusion.23), custom_call_target="Cholesky" | custom-call | tf_op jit(solution)/shard_map/jit(cholesky)/cholesky | solution.py:56
  56.7 3.5 %collective-permute-start = (f32[64,64]{1,0:T(8,128)S(1)}, f32[64,64]{1,0:T(8,128)S(1)}, u32[]{:S(2)}, u32[]{:S(2)}) collective-permute-start(f32[64,64]{1,0:T(8,128)S(1)} %select_select_fusion.6), channel_id=1, source_target_pairs={{0,8},{8,0},{16,24},{24,16},{32,40},{40,32},{48,56},{56,48},{64,72... | collective-permute-start | bytes 49160 | tf_op jit(solution)/shard_map/ppermute | solution.py:15
  60.4 2.1 %collective-permute-done = f32[64,64]{1,0:T(8,128)S(1)} collective-permute-done((f32[64,64]{1,0:T(8,128)S(1)}, f32[64,64]{1,0:T(8,128)S(1)}, u32[]{:S(2)}, u32[]{:S(2)}) %collective-permute-start) | collective-permute-done | bytes 16416 | tf_op jit(solution)/shard_map/ppermute | solution.py:15
  62.8 5.8 %cholesky.130 = f32[64,64]{1,0:T(8,128)S(1)} custom-call(f32[64,64]{1,0:T(8,128)S(1)} %fusion.22), custom_call_target="Cholesky" | custom-call | tf_op jit(solution)/shard_map/jit(cholesky)/cholesky | solution.py:62
  70.0 4.5 %collective-permute-start.1 = (f32[64,64]{1,0:T(8,128)S(1)}, f32[64,64]{1,0:T(8,128)S(1)}, u32[]{:S(2)}, u32[]{:S(2)}) collective-permute-start(f32[64,64]{1,0:T(8,128)S(1)} %select_select_fusion.5), channel_id=1, source_target_pairs={{0,16},{8,24},{16,0},{24,8},{32,48},{40,56},{48,32},{56,40},{64,80... | collective-permute-start | bytes 49160 | tf_op jit(solution)/shard_map/ppermute | solution.py:15
  74.7 2.1 %collective-permute-done.1 = f32[64,64]{1,0:T(8,128)S(1)} collective-permute-done((f32[64,64]{1,0:T(8,128)S(1)}, f32[64,64]{1,0:T(8,128)S(1)}, u32[]{:S(2)}, u32[]{:S(2)}) %collective-permute-start.1) | collective-permute-done | bytes 16416 | tf_op jit(solution)/shard_map/ppermute | solution.py:15
  77.0 5.8 %cholesky.141 = f32[64,64]{1,0:T(8,128)S(1)} custom-call(f32[64,64]{1,0:T(8,128)S(1)} %fusion.21), custom_call_target="Cholesky" | custom-call | tf_op jit(solution)/shard_map/jit(cholesky)/cholesky | solution.py:62
  84.2 7.6 %collective-permute-start.2 = (f32[64,64]{1,0:T(8,128)S(1)}, f32[64,64]{1,0:T(8,128)S(1)}, u32[]{:S(2)}, u32[]{:S(2)}) collective-permute-start(f32[64,64]{1,0:T(8,128)S(1)} %select_select_fusion.4), channel_id=1, source_target_pairs={{0,32},{8,40},{16,48},{24,56},{32,0},{40,8},{48,16},{56,24},{64,96... | collective-permute-start | bytes 49160 | tf_op jit(solution)/shard_map/ppermute | solution.py:15
  92.0 1.9 %collective-permute-done.2 = f32[64,64]{1,0:T(8,128)S(1)} collective-permute-done((f32[64,64]{1,0:T(8,128)S(1)}, f32[64,64]{1,0:T(8,128)S(1)}, u32[]{:S(2)}, u32[]{:S(2)}) %collective-permute-start.2) | collective-permute-done | bytes 16416 | tf_op jit(solution)/shard_map/ppermute | solution.py:15
  94.2 5.8 %cholesky.152 = f32[64,64]{1,0:T(8,128)S(1)} custom-call(f32[64,64]{1,0:T(8,128)S(1)} %fusion.20), custom_call_target="Cholesky" | custom-call | tf_op jit(solution)/shard_map/jit(cholesky)/cholesky | solution.py:62
  101.4 14.0 %collective-permute-start.3 = (f32[64,64]{1,0:T(8,128)S(1)}, f32[64,64]{1,0:T(8,128)S(1)}, u32[]{:S(2)}, u32[]{:S(2)}) collective-permute-start(f32[64,64]{1,0:T(8,128)S(1)} %select_select_fusion.3), channel_id=1, source_target_pairs={{0,64},{8,72},{16,80},{24,88},{32,96},{40,104},{48,112},{56,120},{... | collective-permute-start | bytes 49160 | tf_op jit(solution)/shard_map/ppermute | solution.py:15
  115.6 1.7 %collective-permute-done.3 = f32[64,64]{1,0:T(8,128)S(1)} collective-permute-done((f32[64,64]{1,0:T(8,128)S(1)}, f32[64,64]{1,0:T(8,128)S(1)}, u32[]{:S(2)}, u32[]{:S(2)}) %collective-permute-start.3) | collective-permute-done | bytes 16416 | tf_op jit(solution)/shard_map/ppermute | solution.py:15
  117.6 5.8 %cholesky.163 = f32[64,64]{1,0:T(8,128)S(1)} custom-call(f32[64,64]{1,0:T(8,128)S(1)} %fusion.19), custom_call_target="Cholesky" | custom-call | tf_op jit(solution)/shard_map/jit(cholesky)/cholesky | solution.py:62
  124.8 2.4 %collective-permute-start.4 = (f32[64,64]{1,0:T(8,128)S(1)}, f32[64,64]{1,0:T(8,128)S(1)}, u32[]{:S(2)}, u32[]{:S(2)}) collective-permute-start(f32[64,64]{1,0:T(8,128)S(1)} %select_select_fusion.2), channel_id=1, source_target_pairs={{0,128},{8,136},{16,144},{24,152},{32,160},{40,168},{48,176},{56,1... | collective-permute-start | bytes 49160 | tf_op jit(solution)/shard_map/ppermute | solution.py:15
  127.4 3.2 %collective-permute-done.4 = f32[64,64]{1,0:T(8,128)S(1)} collective-permute-done((f32[64,64]{1,0:T(8,128)S(1)}, f32[64,64]{1,0:T(8,128)S(1)}, u32[]{:S(2)}, u32[]{:S(2)}) %collective-permute-start.4) | collective-permute-done | bytes 16416 | tf_op jit(solution)/shard_map/ppermute | solution.py:15
  130.9 5.8 %cholesky.174 = f32[64,64]{1,0:T(8,128)S(1)} custom-call(f32[64,64]{1,0:T(8,128)S(1)} %fusion.18), custom_call_target="Cholesky" | custom-call | tf_op jit(solution)/shard_map/jit(cholesky)/cholesky | solution.py:62
  138.1 4.0 %collective-permute-start.5 = (f32[64,64]{1,0:T(8,128)S(1)}, f32[64,64]{1,0:T(8,128)S(1)}, u32[]{:S(2)}, u32[]{:S(2)}) collective-permute-start(f32[64,64]{1,0:T(8,128)S(1)} %select_select_fusion.1), channel_id=1, source_target_pairs={{0,256},{8,264},{16,272},{24,280},{32,288},{40,296},{48,304},{56,3... | collective-permute-start | bytes 49160 | tf_op jit(solution)/shard_map/ppermute | solution.py:15
  142.3 3.1 %collective-permute-done.5 = f32[64,64]{1,0:T(8,128)S(1)} collective-permute-done((f32[64,64]{1,0:T(8,128)S(1)}, f32[64,64]{1,0:T(8,128)S(1)}, u32[]{:S(2)}, u32[]{:S(2)}) %collective-permute-start.5) | collective-permute-done | bytes 16416 | tf_op jit(solution)/shard_map/ppermute | solution.py:15
  145.7 5.8 %cholesky.185 = f32[64,64]{1,0:T(8,128)S(1)} custom-call(f32[64,64]{1,0:T(8,128)S(1)} %fusion.17), custom_call_target="Cholesky" | custom-call | tf_op jit(solution)/shard_map/jit(cholesky)/cholesky | solution.py:62
  152.9 4.9 %custom-call.6 = f32[1,64,64]{1,2,0:T(8,128)S(1)} custom-call(f32[1,64,64]{2,1,0:T(8,128)S(1)} %fusion.12), custom_call_target="InvertDiagBlocksLowerTriangular" | custom-call | tf_op jit(solution)/shard_map/jit(_solve_triangular)/triangular_solve | solution.py:63
  (69 shorter events, 15.2 us)
Async XLA Ops:
  6.5 3.8 %copy-start = (bf16[128,1024]{1,0:T(8,128)(2,1)S(1)}, bf16[128,1024]{1,0:T(8,128)(2,1)}, u32[]{:S(2)}) copy-start(bf16[128,1024]{1,0:T(8,128)(2,1)} %param.8) | copy-start | bytes 786436
  6.5 2.7 %copy-start.4 = (bf16[3584,128]{1,0:T(8,128)(2,1)S(1)}, bf16[3584,128]{1,0:T(8,128)(2,1)}, u32[]{:S(2)}) copy-start(bf16[3584,128]{1,0:T(8,128)(2,1)} %param.14) | copy-start | bytes 2752516
  6.5 2.7 %copy-start.5 = (bf16[128,3584]{1,0:T(8,128)(2,1)S(1)}, bf16[128,3584]{1,0:T(8,128)(2,1)}, u32[]{:S(2)}) copy-start(bf16[128,3584]{1,0:T(8,128)(2,1)} %param.9) | copy-start | bytes 2752516
  6.5 2.7 %copy-start.3 = (bf16[128,3584]{1,0:T(8,128)(2,1)S(1)}, bf16[128,3584]{1,0:T(8,128)(2,1)}, u32[]{:S(2)}) copy-start(bf16[128,3584]{1,0:T(8,128)(2,1)} %param.10) | copy-start | bytes 2752516
  6.5 40.6 %all-gather.3.cloned.1.call-start = ((), (), s32[]{:S(2)}) async-start(), calls=%async_computation | async-start | bytes 1179648 | tf_op jit(solution)/shard_map/all_gather | solution.py:51
  9.3 1.0 copy-start.1
  9.3 1.3 copy-start.2
  56.7 5.8 %collective-permute-start = (f32[64,64]{1,0:T(8,128)S(1)}, f32[64,64]{1,0:T(8,128)S(1)}, u32[]{:S(2)}, u32[]{:S(2)}) collective-permute-start(f32[64,64]{1,0:T(8,128)S(1)} %select_select_fusion.6), channel_id=1, source_target_pairs={{0,8},{8,0},{16,24},{24,16},{32,40},{40,32},{48,56},{56,48},{64,72... | collective-permute-start | bytes 49160 | tf_op jit(solution)/shard_map/ppermute | solution.py:15
  70.0 6.7 %collective-permute-start.1 = (f32[64,64]{1,0:T(8,128)S(1)}, f32[64,64]{1,0:T(8,128)S(1)}, u32[]{:S(2)}, u32[]{:S(2)}) collective-permute-start(f32[64,64]{1,0:T(8,128)S(1)} %select_select_fusion.5), channel_id=1, source_target_pairs={{0,16},{8,24},{16,0},{24,8},{32,48},{40,56},{48,32},{56,40},{64,80... | collective-permute-start | bytes 49160 | tf_op jit(solution)/shard_map/ppermute | solution.py:15
  84.2 9.7 %collective-permute-start.2 = (f32[64,64]{1,0:T(8,128)S(1)}, f32[64,64]{1,0:T(8,128)S(1)}, u32[]{:S(2)}, u32[]{:S(2)}) collective-permute-start(f32[64,64]{1,0:T(8,128)S(1)} %select_select_fusion.4), channel_id=1, source_target_pairs={{0,32},{8,40},{16,48},{24,56},{32,0},{40,8},{48,16},{56,24},{64,96... | collective-permute-start | bytes 49160 | tf_op jit(solution)/shard_map/ppermute | solution.py:15
  101.4 15.9 %collective-permute-start.3 = (f32[64,64]{1,0:T(8,128)S(1)}, f32[64,64]{1,0:T(8,128)S(1)}, u32[]{:S(2)}, u32[]{:S(2)}) collective-permute-start(f32[64,64]{1,0:T(8,128)S(1)} %select_select_fusion.3), channel_id=1, source_target_pairs={{0,64},{8,72},{16,80},{24,88},{32,96},{40,104},{48,112},{56,120},{... | collective-permute-start | bytes 49160 | tf_op jit(solution)/shard_map/ppermute | solution.py:15
  124.8 5.8 %collective-permute-start.4 = (f32[64,64]{1,0:T(8,128)S(1)}, f32[64,64]{1,0:T(8,128)S(1)}, u32[]{:S(2)}, u32[]{:S(2)}) collective-permute-start(f32[64,64]{1,0:T(8,128)S(1)} %select_select_fusion.2), channel_id=1, source_target_pairs={{0,128},{8,136},{16,144},{24,152},{32,160},{40,168},{48,176},{56,1... | collective-permute-start | bytes 49160 | tf_op jit(solution)/shard_map/ppermute | solution.py:15
  138.1 7.3 %collective-permute-start.5 = (f32[64,64]{1,0:T(8,128)S(1)}, f32[64,64]{1,0:T(8,128)S(1)}, u32[]{:S(2)}, u32[]{:S(2)}) collective-permute-start(f32[64,64]{1,0:T(8,128)S(1)} %select_select_fusion.1), channel_id=1, source_target_pairs={{0,256},{8,264},{16,272},{24,280},{32,288},{40,296},{48,304},{56,3... | collective-permute-start | bytes 49160 | tf_op jit(solution)/shard_map/ppermute | solution.py:15
Sparse Core Ops, SparseCore 0:
  11.8 35.2 all-gather.2
